TPU v7x, 32 devices: a whole 2x2x4 slice. The times are simulated.
32 devices in a mesh: section: 2 (over x), row: 4 (over y, core), col: 4 (over z).
Axes of the slice: x: 2, y: 2, z: 4, core: 2. Of those that a mesh axis runs over, the one named last changes fastest.
Arguments:
- layer_input: bfloat16 [2, 2, 128, 8192], P('section', None, 'col', 'row'), may hold values from -6 to 6
- top_grad: bfloat16 [2, 128, 8192], P(None, 'col', 'row'), may hold values from -6 to 6
- gate_weight: bfloat16 [2, 8192, 14336], P('section', 'row', 'col'), may hold values from -0.0625 to 0.0625
- up_weight: bfloat16 [2, 8192, 14336], P('section', 'row', 'col'), may hold values from -0.0625 to 0.0625
- down_weight: bfloat16 [2, 14336, 8192], P('section', 'col', 'row'), may hold values from -0.046875 to 0.046875
- activity: int32 [2, 2, 2, 4, 28], P('section', None, None, 'col'), may hold values from 0 to 56, as said below
Outputs:
- sent_grad: bfloat16 [2, 2, 128, 8192], P('section', None, 'col', 'row')
- gate_grad: bfloat16 [2, 8192, 14336], P('section', 'row', 'col')
- up_grad: bfloat16 [2, 8192, 14336], P('section', 'row', 'col')
- down_grad: bfloat16 [2, 14336, 8192], P('section', 'col', 'row')
Inputs may be any that keep to these rules, and one draw needn't show every extreme that they name: `activity`: each list names distinct blocks below 56, then the value 56 marks empty slots up to the end; every list holds at least 7 blocks, and in every token block some column's list is full.
All inputs are finite; a program needn't handle non-finite values.
Results may differ from a plain program's by a relative error of at most 0.006.
Values may be sent and summed in bfloat16 or wider, within the bound.
No kernel may reach another device: no remote copies, remote signals or barrier semaphores. Data moves between devices by JAX's collectives and lax.ppermute only.
A program may use at most 384 MiB of HBM per device.

v0:
```python
import jax
import jax.numpy as jnp
from jax import lax
from jax.sharding import PartitionSpec as P

BLK = 64
TB = 64


def passed_along(value, axis, steps):
    count = lax.axis_size(axis)
    initial, last = (max(0, -steps), min(count, count - steps))
    return lax.ppermute(value, axis, [(source, source + steps) for source in range(initial, last)])


def activate(gate_total, up_total, grad_total, keep_mask):
    positive = jnp.maximum(gate_total, 0.0)
    squared = keep_mask * positive * positive
    hidden = (squared * up_total).astype(jnp.bfloat16)
    grad_up = (squared * grad_total).astype(jnp.bfloat16)
    grad_hgate = (keep_mask * 2.0 * positive * up_total * grad_total).astype(jnp.bfloat16)
    return (hidden, grad_hgate, grad_up)


def combine(gate_part, up_part, grad_part, keep_mask):
    gate_total, up_total, grad_total = (
        lax.psum_scatter(gate_part, "row", scatter_dimension=0, tiled=True),
        lax.psum_scatter(up_part, "row", scatter_dimension=0, tiled=True),
        lax.psum_scatter(grad_part, "row", scatter_dimension=0, tiled=True),
    )
    row_count = gate_total.shape[0]
    own_mask = lax.dynamic_slice_in_dim(keep_mask, lax.axis_index("row") * row_count, row_count, 0)
    results = activate(gate_total, up_total, grad_total, own_mask)
    hidden, grad_hgate, grad_up = (
        lax.all_gather(results[0], "row", axis=0, tiled=True),
        lax.all_gather(results[1], "row", axis=0, tiled=True),
        lax.all_gather(results[2], "row", axis=0, tiled=True),
    )
    return (hidden, grad_hgate, grad_up)


def shards(layer_input, top_grad, gate_weight, up_weight, down_weight, activity):
    sections = lax.axis_size("section")
    section_pos = lax.axis_index("section")
    inputs_all = layer_input[0]
    w_gate = gate_weight[0]
    w_up = up_weight[0]
    w_down = down_weight[0]
    lists_all = activity[0, :, :, 0, :]
    micro_count = inputs_all.shape[0]
    block_total = w_gate.shape[1] // BLK
    sum_gate = jnp.zeros(w_gate.shape, jnp.float32)
    sum_up = jnp.zeros(w_up.shape, jnp.float32)
    sum_down = jnp.zeros(w_down.shape, jnp.float32)
    sent = jnp.zeros(layer_input.shape, jnp.bfloat16)
    received = jnp.zeros(inputs_all.shape[1:], jnp.bfloat16)
    for tick_number in range(micro_count + sections - 1):
        micro_pos = tick_number - (sections - 1 - section_pos)
        usable = jnp.logical_and(micro_pos >= 0, micro_pos < micro_count)
        chosen = jnp.clip(micro_pos, 0, micro_count - 1)
        active_flag = usable.astype(jnp.float32)
        local_input = lax.dynamic_index_in_dim(inputs_all, chosen, 0, keepdims=False)
        top_local = lax.dynamic_index_in_dim(top_grad, chosen, 0, keepdims=False)
        grad_in = jnp.where(section_pos == sections - 1, top_local, received)
        rows_input, rows_grad = (
            lax.all_gather(local_input, "col", axis=0, tiled=True),
            lax.all_gather(grad_in, "col", axis=0, tiled=True),
        )
        block_list = lax.dynamic_index_in_dim(lists_all, chosen, 0, keepdims=False)
        tokens = rows_input.shape[0]
        block_count = tokens // TB
        blocks = jnp.arange(block_total, dtype=jnp.int32)
        block_on = (
            jnp.any(block_list[:, :, None] == blocks[None, None, :], axis=1).astype(jnp.float32)
            * active_flag
        )
        keep_mask = jnp.broadcast_to(
            block_on[:, None, :, None], (block_count, TB, block_total, BLK)
        ).reshape(tokens, block_total * BLK)
        gate_part = jnp.dot(rows_input, w_gate, preferred_element_type=jnp.float32)
        up_part = jnp.dot(rows_input, w_up, preferred_element_type=jnp.float32)
        grad_part = jnp.einsum("td,fd->tf", rows_grad, w_down, preferred_element_type=jnp.float32)
        hidden, grad_hgate, grad_up = combine(gate_part, up_part, grad_part, keep_mask)
        sum_gate = sum_gate + jnp.einsum(
            "td,tf->df", rows_input, grad_hgate, preferred_element_type=jnp.float32
        )
        sum_up = sum_up + jnp.einsum(
            "td,tf->df", rows_input, grad_up, preferred_element_type=jnp.float32
        )
        sum_down = sum_down + jnp.einsum(
            "tf,td->fd", hidden, rows_grad, preferred_element_type=jnp.float32
        )
        partial_back = jnp.einsum(
            "tf,df->td", grad_hgate, w_gate, preferred_element_type=jnp.float32
        )
        partial_back = partial_back + jnp.einsum(
            "tf,df->td", grad_up, w_up, preferred_element_type=jnp.float32
        )
        summed = lax.psum_scatter(partial_back, "col", scatter_dimension=0, tiled=True)
        handed = (grad_in.astype(jnp.float32) + summed).astype(jnp.bfloat16)
        written = lax.dynamic_update_slice(sent, handed[None, None], (0, chosen, 0, 0))
        sent = jnp.where(usable, written, sent)
        received = passed_along(handed, "section", -1)
    return (
        sent,
        sum_gate.astype(jnp.bfloat16)[None],
        sum_up.astype(jnp.bfloat16)[None],
        sum_down.astype(jnp.bfloat16)[None],
    )


def solution(mesh):
    in_specs = (
        P("section", None, "col", "row"),
        P(None, "col", "row"),
        P("section", "row", "col"),
        P("section", "row", "col"),
        P("section", "col", "row"),
        P("section", None, None, "col", None),
    )
    out_specs = (
        P("section", None, "col", "row"),
        P("section", "row", "col"),
        P("section", "row", "col"),
        P("section", "col", "row"),
    )
    return jax.shard_map(shards, mesh=mesh, in_specs=in_specs, out_specs=out_specs, check_vma=False)
```

profile of v0, /device:TPU:3, one launch (start us, length us, event | category | flops | bytes accessed | tf_op | source)
XLA Modules:
  0.0 651.4 jit_solution(17873560761817971865)
XLA Ops:
  8.9 14.5 %all-gather = bf16[1,1,128,2048]{3,2,1,0:T(8,128)(2,1)S(1)} all-gather(bf16[1,1,32,2048]{3,2,1,0:T(8,128)(2,1)S(1)} %get-tuple-element.18), channel_id=2, replica_groups=mesh['section'=2,'row'=4,'col'=4] {'col'}, dimensions={2}, use_global_device_ids=true | all-gather | bytes 655360 | tf_op jit(solution)/shard_map/all_gather | solution.py:66
  23.4 8.5 %fusion.16 = f32[128,3584]{1,0:T(8,128)} fusion(bf16[1,2048,3584]{2,1,0:T(8,128)(2,1)} %param.9, bf16[1,1,128,2048]{3,2,1,0:T(8,128)(2,1)S(1)} %all-gather), kind=kOutput, calls=%fused_computation.19 | convolution fusion | flops 1879048192 | bytes 17039360 | tf_op jit(solution)/shard_map/dot_general | solution.py:81
  32.0 8.5 %fusion.28 = f32[128,3584]{1,0:T(8,128)} fusion(bf16[1,2048,3584]{2,1,0:T(8,128)(2,1)} %param.8, bf16[1,1,128,2048]{3,2,1,0:T(8,128)(2,1)S(1)} %all-gather), kind=kOutput, calls=%fused_computation.31 | convolution fusion | flops 1879048192 | bytes 17039360 | tf_op jit(solution)/shard_map/dot_general | solution.py:80
  40.6 11.9 %all-gather.1 = bf16[1,128,2048]{2,1,0:T(8,128)(2,1)S(1)} all-gather(bf16[1,32,2048]{2,1,0:T(8,128)(2,1)S(1)} %dynamic-slice_select_fusion), channel_id=3, replica_groups=mesh['section'=2,'row'=4,'col'=4] {'col'}, dimensions={1}, use_global_device_ids=true | all-gather | bytes 655360 | tf_op jit(solution)/shard_map/all_gather | solution.py:67
  53.3 11.4 %fusion.4 = f32[128,3584]{1,0:T(8,128)} fusion(bf16[1,3584,2048]{2,1,0:T(8,128)(2,1)} %param.10, bf16[1,128,2048]{2,1,0:T(8,128)(2,1)S(1)} %all-gather.1), kind=kOutput, calls=%fused_computation.7 | convolution fusion | flops 1879048192 | bytes 17039360 | tf_op jit(solution)/shard_map/td,fd->tf/dot_general | solution.py:82
  67.1 3.0 reshape.48
  70.1 27.3 %reduce-scatter.13.cloned.1.call-done = f32[32,3584]{1,0:T(8,128)} async-done(((f32[128,3584]{1,0:T(8,128)}), f32[32,3584]{1,0:T(8,128)}) %reduce-scatter.13.cloned.1.call-update) | async-done | bytes 458768 | tf_op jit(solution)/shard_map/reduce_scatter | solution.py:27
  97.4 32.2 %reduce-scatter.17.cloned.1.call-done = f32[32,3584]{1,0:T(8,128)} async-done(((f32[128,3584]{1,0:T(8,128)}), f32[32,3584]{1,0:T(8,128)}) %reduce-scatter.17.cloned.1.call-update) | async-done | bytes 458768 | tf_op jit(solution)/shard_map/reduce_scatter | solution.py:29
  131.7 9.4 %all_gather.48 = bf16[128,3584]{1,0:T(8,128)(2,1)S(1)} all-gather(bf16[32,3584]{1,0:T(8,128)(2,1)S(1)} %get-tuple-element.13), channel_id=1, replica_groups=mesh['section'=2,'row'=4,'col'=4] {'row'}, dimensions={0}, use_global_device_ids=true | all-gather | bytes 1146880 | tf_op jit(solution)/shard_map/all_gather | solution.py:37
  141.1 9.9 %fusion.14 = f32[128,2048]{1,0:T(8,128)S(1)} fusion(bf16[128,3584]{1,0:T(8,128)(2,1)S(1)} %all_gather.48, bf16[1,2048,3584]{2,1,0:T(8,128)(2,1)} %param.9), kind=kOutput, calls=%fused_computation.17 | convolution fusion | flops 1879048192 | bytes 16646144 | tf_op jit(solution)/shard_map/tf,df->td/dot_general | solution.py:96
  151.0 9.6 %all_gather.47 = bf16[128,3584]{1,0:T(8,128)(2,1)S(1)} all-gather(bf16[32,3584]{1,0:T(8,128)(2,1)S(1)} %get-tuple-element.12), channel_id=1, replica_groups=mesh['section'=2,'row'=4,'col'=4] {'row'}, dimensions={0}, use_global_device_ids=true | all-gather | bytes 1146880 | tf_op jit(solution)/shard_map/all_gather | solution.py:36
  160.6 10.9 %fusion.33 = f32[128,2048]{1,0:T(8,128)} fusion(f32[128,2048]{1,0:T(8,128)S(1)} %fusion.14, bf16[128,3584]{1,0:T(8,128)(2,1)S(1)} %all_gather.47, bf16[1,2048,3584]{2,1,0:T(8,128)(2,1)} %param.8), kind=kOutput, calls=%fused_computation.36 | convolution fusion | flops 1879310336 | bytes 17694720 | tf_op jit(solution)/shard_map/tf,df->td/dot_general | solution.py:93
  171.6 17.7 %all-gather.2 = bf16[1,1,128,2048]{3,2,1,0:T(8,128)(2,1)S(1)} all-gather(bf16[1,1,32,2048]{3,2,1,0:T(8,128)(2,1)S(1)} %get-tuple-element.19), channel_id=4, replica_groups=mesh['section'=2,'row'=4,'col'=4] {'col'}, dimensions={2}, use_global_device_ids=true | all-gather | bytes 655360 | tf_op jit(solution)/shard_map/all_gather | solution.py:66
  189.4 8.5 %fusion.12 = f32[128,3584]{1,0:T(8,128)} fusion(bf16[1,2048,3584]{2,1,0:T(8,128)(2,1)} %param.9, bf16[1,1,128,2048]{3,2,1,0:T(8,128)(2,1)S(1)} %all-gather.2), kind=kOutput, calls=%fused_computation.15 | convolution fusion | flops 1879048192 | bytes 17039360 | tf_op jit(solution)/shard_map/dot_general | solution.py:81
  198.0 8.6 %fusion.24 = f32[128,3584]{1,0:T(8,128)} fusion(bf16[1,2048,3584]{2,1,0:T(8,128)(2,1)} %param.8, bf16[1,1,128,2048]{3,2,1,0:T(8,128)(2,1)S(1)} %all-gather.2), kind=kOutput, calls=%fused_computation.27 | convolution fusion | flops 1879048192 | bytes 17039360 | tf_op jit(solution)/shard_map/dot_general | solution.py:80
  207.7 2.3 collective-permute-start
  212.0 13.8 %all_gather.50 = bf16[128,2048]{1,0:T(8,128)(2,1)S(1)} all-gather(bf16[32,2048]{1,0:T(8,128)(2,1)S(1)} %bitcast_select_fusion.2), channel_id=1, replica_groups=mesh['section'=2,'row'=4,'col'=4] {'col'}, dimensions={0}, use_global_device_ids=true | all-gather | bytes 655360 | tf_op jit(solution)/shard_map/all_gather | solution.py:67
  225.8 11.6 %fusion.2 = f32[128,3584]{1,0:T(8,128)} fusion(bf16[128,2048]{1,0:T(8,128)(2,1)S(1)} %all_gather.50, bf16[1,3584,2048]{2,1,0:T(8,128)(2,1)} %param.10), kind=kOutput, calls=%fused_computation.5 | convolution fusion | flops 1879048192 | bytes 17039360 | tf_op jit(solution)/shard_map/td,fd->tf/dot_general | solution.py:82
  239.7 4.0 reshape.49
  243.7 24.6 %reduce-scatter.21.cloned.1.call-done = f32[32,3584]{1,0:T(8,128)} async-done(((f32[128,3584]{1,0:T(8,128)}), f32[32,3584]{1,0:T(8,128)}) %reduce-scatter.21.cloned.1.call-update) | async-done | bytes 458768 | tf_op jit(solution)/shard_map/reduce_scatter | solution.py:27
  268.3 32.1 %reduce-scatter.25.cloned.1.call-done = f32[32,3584]{1,0:T(8,128)} async-done(((f32[128,3584]{1,0:T(8,128)}), f32[32,3584]{1,0:T(8,128)}) %reduce-scatter.25.cloned.1.call-update) | async-done | bytes 458768 | tf_op jit(solution)/shard_map/reduce_scatter | solution.py:29
  302.7 9.8 %all_gather.52 = bf16[128,3584]{1,0:T(8,128)(2,1)S(1)} all-gather(bf16[32,3584]{1,0:T(8,128)(2,1)S(1)} %get-tuple-element.10), channel_id=1, replica_groups=mesh['section'=2,'row'=4,'col'=4] {'row'}, dimensions={0}, use_global_device_ids=true | all-gather | bytes 1146880 | tf_op jit(solution)/shard_map/all_gather | solution.py:37
  313.5 9.9 %fusion.10 = f32[128,2048]{1,0:T(8,128)S(1)} fusion(bf16[128,3584]{1,0:T(8,128)(2,1)S(1)} %all_gather.52, bf16[1,2048,3584]{2,1,0:T(8,128)(2,1)} %param.9), kind=kOutput, calls=%fused_computation.13 | convolution fusion | flops 1879048192 | bytes 16646144 | tf_op jit(solution)/shard_map/tf,df->td/dot_general | solution.py:96
  323.4 9.4 %all_gather.51 = bf16[128,3584]{1,0:T(8,128)(2,1)S(1)} all-gather(bf16[32,3584]{1,0:T(8,128)(2,1)S(1)} %get-tuple-element.9), channel_id=1, replica_groups=mesh['section'=2,'row'=4,'col'=4] {'row'}, dimensions={0}, use_global_device_ids=true | all-gather | bytes 1146880 | tf_op jit(solution)/shard_map/all_gather | solution.py:36
  333.8 11.0 %fusion.36 = f32[128,2048]{1,0:T(8,128)} fusion(f32[128,2048]{1,0:T(8,128)S(1)} %fusion.10, bf16[128,3584]{1,0:T(8,128)(2,1)S(1)} %all_gather.51, bf16[1,2048,3584]{2,1,0:T(8,128)(2,1)} %param.8), kind=kOutput, calls=%fused_computation.37 | convolution fusion | flops 1879310336 | bytes 17694720 | tf_op jit(solution)/shard_map/tf,df->td/dot_general | solution.py:93
  344.9 18.2 %all-gather.3 = bf16[1,1,128,2048]{3,2,1,0:T(8,128)(2,1)S(1)} all-gather(bf16[1,1,32,2048]{3,2,1,0:T(8,128)(2,1)} %get-tuple-element.17), channel_id=5, replica_groups=mesh['section'=2,'row'=4,'col'=4] {'col'}, dimensions={2}, use_global_device_ids=true | all-gather | bytes 655360 | tf_op jit(solution)/shard_map/all_gather | solution.py:66
  363.1 8.5 %fusion.8 = f32[128,3584]{1,0:T(8,128)} fusion(bf16[1,2048,3584]{2,1,0:T(8,128)(2,1)} %param.9, bf16[1,1,128,2048]{3,2,1,0:T(8,128)(2,1)S(1)} %all-gather.3), kind=kOutput, calls=%fused_computation.11 | convolution fusion | flops 1879048192 | bytes 17039360 | tf_op jit(solution)/shard_map/dot_general | solution.py:81
  371.7 8.6 %fusion.20 = f32[128,3584]{1,0:T(8,128)} fusion(bf16[1,2048,3584]{2,1,0:T(8,128)(2,1)} %param.8, bf16[1,1,128,2048]{3,2,1,0:T(8,128)(2,1)S(1)} %all-gather.3), kind=kOutput, calls=%fused_computation.23 | convolution fusion | flops 1879048192 | bytes 17039360 | tf_op jit(solution)/shard_map/dot_general | solution.py:80
  382.6 4.0 reshape.50
  386.6 12.6 %all_gather.57 = bf16[128,3584]{1,0:T(8,128)(2,1)S(1)} all-gather(bf16[32,3584]{1,0:T(8,128)(2,1)} %get-tuple-element.11), channel_id=1, replica_groups=mesh['section'=2,'row'=4,'col'=4] {'row'}, dimensions={0}, use_global_device_ids=true | all-gather | bytes 1146880 | tf_op jit(solution)/shard_map/all_gather | solution.py:35
  399.3 12.7 %fusion.52 = f32[3584,2048]{1,0:T(8,128)} fusion(bf16[128,3584]{1,0:T(8,128)(2,1)S(1)} %all_gather.57, bf16[1,128,2048]{2,1,0:T(8,128)(2,1)} %copy-done.4), kind=kOutput, calls=%fused_computation.52 | convolution fusion | flops 1879048192 | bytes 30801920 | tf_op jit(solution)/shard_map/tf,td->fd/dot_general | solution.py:90
  412.0 12.3 %fusion.57 = f32[2048,3584]{1,0:T(8,128)} fusion(bf16[128,3584]{1,0:T(8,128)(2,1)S(1)} %all_gather.47, bf16[1,1,128,2048]{3,2,1,0:T(8,128)(2,1)S(1)} %all-gather), kind=kOutput, calls=%fused_computation.57 | convolution fusion | flops 1879048192 | bytes 30801920 | tf_op jit(solution)/shard_map/td,tf->df/dot_general | solution.py:84
  426.1 2.3 collective-permute-start.1
  428.4 12.0 %fusion.55 = f32[2048,3584]{1,0:T(8,128)} fusion(bf16[128,3584]{1,0:T(8,128)(2,1)S(1)} %all_gather.48, bf16[1,1,128,2048]{3,2,1,0:T(8,128)(2,1)S(1)} %all-gather), kind=kOutput, calls=%fused_computation.55 | convolution fusion | flops 1879048192 | bytes 30801920 | tf_op jit(solution)/shard_map/td,tf->df/dot_general | solution.py:87
  440.4 13.6 %all_gather.54 = bf16[128,2048]{1,0:T(8,128)(2,1)S(1)} all-gather(bf16[32,2048]{1,0:T(8,128)(2,1)S(1)} %bitcast_select_fusion), channel_id=1, replica_groups=mesh['section'=2,'row'=4,'col'=4] {'col'}, dimensions={0}, use_global_device_ids=true | all-gather | bytes 655360 | tf_op jit(solution)/shard_map/all_gather | solution.py:67
  454.0 11.5 %fusion = f32[128,3584]{1,0:T(8,128)} fusion(bf16[128,2048]{1,0:T(8,128)(2,1)S(1)} %all_gather.54, bf16[1,3584,2048]{2,1,0:T(8,128)(2,1)} %param.10), kind=kOutput, calls=%fused_computation.3 | convolution fusion | flops 1879048192 | bytes 17039360 | tf_op jit(solution)/shard_map/td,fd->tf/dot_general | solution.py:82
  465.8 12.4 %fusion.48 = f32[2048,3584]{1,0:T(8,128)} fusion(bf16[128,3584]{1,0:T(8,128)(2,1)S(1)} %copy-done.3, bf16[1,1,128,2048]{3,2,1,0:T(8,128)(2,1)S(1)} %all-gather.2), kind=kOutput, calls=%fused_computation.48 | convolution fusion | flops 1879048192 | bytes 30801920 | tf_op jit(solution)/shard_map/td,tf->df/dot_general | solution.py:84
  478.1 14.8 %all_gather.58 = bf16[128,3584]{1,0:T(8,128)(2,1)S(1)} all-gather(bf16[32,3584]{1,0:T(8,128)(2,1)S(1)} %copy-done.15), channel_id=1, replica_groups=mesh['section'=2,'row'=4,'col'=4] {'row'}, dimensions={0}, use_global_device_ids=true | all-gather | bytes 1146880 | tf_op jit(solution)/shard_map/all_gather | solution.py:35
  492.9 11.9 %fusion.46 = f32[2048,3584]{1,0:T(8,128)} fusion(bf16[128,3584]{1,0:T(8,128)(2,1)S(1)} %copy-done.1, bf16[1,1,128,2048]{3,2,1,0:T(8,128)(2,1)S(1)} %all-gather.2), kind=kOutput, calls=%fused_computation.46 | convolution fusion | flops 1879048192 | bytes 30801920 | tf_op jit(solution)/shard_map/td,tf->df/dot_general | solution.py:87
  504.8 11.6 %fusion.70 = f32[3584,2048]{1,0:T(8,128)} fusion(bf16[128,3584]{1,0:T(8,128)(2,1)S(1)} %all_gather.58, bf16[128,2048]{1,0:T(8,128)(2,1)S(1)} %copy-done.6), kind=kOutput, calls=%fused_computation.98 | convolution fusion | flops 1879048192 | bytes 30801920 | tf_op jit(solution)/shard_map/tf,td->fd/dot_general | solution.py:90
  518.0 9.4 %all_gather.56 = bf16[128,3584]{1,0:T(8,128)(2,1)S(1)} all-gather(bf16[32,3584]{1,0:T(8,128)(2,1)S(1)} %get-tuple-element.16), channel_id=1, replica_groups=mesh['section'=2,'row'=4,'col'=4] {'row'}, dimensions={0}, use_global_device_ids=true | all-gather | bytes 1146880 | tf_op jit(solution)/shard_map/all_gather | solution.py:37
  527.4 9.9 %fusion.6 = f32[128,2048]{1,0:T(8,128)S(1)} fusion(bf16[128,3584]{1,0:T(8,128)(2,1)S(1)} %all_gather.56, bf16[1,2048,3584]{2,1,0:T(8,128)(2,1)} %param.9), kind=kOutput, calls=%fused_computation.9 | convolution fusion | flops 1879048192 | bytes 16646144 | tf_op jit(solution)/shard_map/tf,df->td/dot_general | solution.py:96
  537.3 9.4 %all_gather.55 = bf16[128,3584]{1,0:T(8,128)(2,1)S(1)} all-gather(bf16[32,3584]{1,0:T(8,128)(2,1)S(1)} %get-tuple-element.15), channel_id=1, replica_groups=mesh['section'=2,'row'=4,'col'=4] {'row'}, dimensions={0}, use_global_device_ids=true | all-gather | bytes 1146880 | tf_op jit(solution)/shard_map/all_gather | solution.py:36
  546.7 10.9 %fusion.39 = f32[128,2048]{1,0:T(8,128)} fusion(f32[128,2048]{1,0:T(8,128)S(1)} %fusion.6, bf16[128,3584]{1,0:T(8,128)(2,1)S(1)} %all_gather.55, bf16[1,2048,3584]{2,1,0:T(8,128)(2,1)} %param.8), kind=kOutput, calls=%fused_computation.38 | convolution fusion | flops 1879310336 | bytes 17694720 | tf_op jit(solution)/shard_map/tf,df->td/dot_general | solution.py:93
  557.6 9.7 %all_gather.59 = bf16[128,3584]{1,0:T(8,128)(2,1)S(1)} all-gather(bf16[32,3584]{1,0:T(8,128)(2,1)S(1)} %get-tuple-element.14), channel_id=1, replica_groups=mesh['section'=2,'row'=4,'col'=4] {'row'}, dimensions={0}, use_global_device_ids=true | all-gather | bytes 1146880 | tf_op jit(solution)/shard_map/all_gather | solution.py:35
  567.3 25.2 %fusion.30 = bf16[1,2048,3584]{2,1,0:T(8,128)(2,1)} fusion(bf16[128,3584]{1,0:T(8,128)(2,1)S(1)} %all_gather.55, f32[2048,3584]{1,0:T(8,128)} %fusion.57, f32[2048,3584]{1,0:T(8,128)} %fusion.48, bf16[1,1,128,2048]{3,2,1,0:T(8,128)(2,1)S(1)} %all-gather.3), kind=kOutput, calls=%fused_computation.33 | convolution fusion | flops 1901068288 | bytes 74842112 | tf_op jit(solution)/shard_map/td,tf->df/dot_general | solution.py:84
  592.5 24.9 %fusion.32 = bf16[1,3584,2048]{2,1,0:T(8,128)(2,1)} fusion(bf16[128,3584]{1,0:T(8,128)(2,1)S(1)} %all_gather.59, bf16[128,2048]{1,0:T(8,128)(2,1)S(1)} %copy-done.8, f32[3584,2048]{1,0:T(8,128)} %fusion.52, f32[3584,2048]{1,0:T(8,128)} %fusion.70), kind=kOutput, calls=%fused_computation.35 | convolution fusion | flops 1901068288 | bytes 74842112 | tf_op jit(solution)/shard_map/tf,td->fd/dot_general | solution.py:90
  617.4 25.0 %fusion.31 = bf16[1,2048,3584]{2,1,0:T(8,128)(2,1)} fusion(bf16[128,3584]{1,0:T(8,128)(2,1)S(1)} %all_gather.56, f32[2048,3584]{1,0:T(8,128)} %fusion.55, f32[2048,3584]{1,0:T(8,128)} %fusion.46, bf16[1,1,128,2048]{3,2,1,0:T(8,128)(2,1)S(1)} %all-gather.3), kind=kOutput, calls=%fused_computation.34 | convolution fusion | flops 1901068288 | bytes 74842112 | tf_op jit(solution)/shard_map/td,tf->df/dot_general | solution.py:87
  (89 shorter events, 24.6 us)
Async XLA Ops:
  7.2 62.9 %reduce-scatter.15.cloned.1.call-start = ((), (), s32[]{:S(2)}) async-start(), calls=%async_computation.13 | async-start | bytes 2293760 | tf_op jit(solution)/shard_map/reduce_scatter | solution.py:28
  31.9 8.6 %copy-start.9 = (bf16[2,32,2048]{2,1,0:T(8,128)(2,1)S(1)}, bf16[2,32,2048]{2,1,0:T(8,128)(2,1)}, u32[]{:S(2)}) copy-start(bf16[2,32,2048]{2,1,0:T(8,128)(2,1)} %param.7) | copy-start | bytes 786436
  31.9 65.4 %reduce-scatter.13.cloned.1.call-start = ((), (), s32[]{:S(2)}) async-start(), calls=%async_computation.12 | async-start | bytes 2293760 | tf_op jit(solution)/shard_map/reduce_scatter | solution.py:27
  40.5 24.3 %copy-start.16 = (s32[1,2,2,1,28]{4,3,2,1,0:T(1,128)S(1)}, s32[1,2,2,1,28]{4,3,2,1,0:T(1,128)}, u32[]{:S(2)}) copy-start(s32[1,2,2,1,28]{4,3,2,1,0:T(1,128)} %param.11) | copy-start | bytes 1348
  40.5 89.1 %reduce-scatter.17.cloned.1.call-start = ((), (), s32[]{:S(2)}) async-start(), calls=%async_computation.14 | async-start | bytes 2293760 | tf_op jit(solution)/shard_map/reduce_scatter | solution.py:29
  52.5 0.8 copy-start.4
  64.7 141.9 %reduce-scatter.19.cloned.1.call-start = ((), (), s32[]{:S(2)}) async-start(), calls=%async_computation.15 | async-start | bytes 1310720 | tf_op jit(solution)/shard_map/reduce_scatter | solution.py:99
  171.6 72.1 %reduce-scatter.23.cloned.1.call-start = ((), (), s32[]{:S(2)}) async-start(), calls=%async_computation.17 | async-start | bytes 2293760 | tf_op jit(solution)/shard_map/reduce_scatter | solution.py:28
  197.9 8.8 %copy-start.10 = (bf16[2,32,2048]{2,1,0:T(8,128)(2,1)S(1)}, bf16[2,32,2048]{2,1,0:T(8,128)(2,1)}, u32[]{:S(2)}) copy-start(bf16[2,32,2048]{2,1,0:T(8,128)(2,1)} %param.7) | copy-start | bytes 786436
  197.9 70.4 %reduce-scatter.21.cloned.1.call-start = ((), (), s32[]{:S(2)}) async-start(), calls=%async_computation.16 | async-start | bytes 2293760 | tf_op jit(solution)/shard_map/reduce_scatter | solution.py:27
  206.6 93.9 %reduce-scatter.25.cloned.1.call-start = ((), (), s32[]{:S(2)}) async-start(), calls=%async_computation.18 | async-start | bytes 2293760 | tf_op jit(solution)/shard_map/reduce_scatter | solution.py:29
  207.7 4.3 copy-start.12
  207.7 4.3 collective-permute-start
  225.8 76.9 %copy-start.5 = (bf16[128,2048]{1,0:T(8,128)(2,1)}, bf16[128,2048]{1,0:T(8,128)(2,1)S(1)}, u32[]{:S(2)}) copy-start(bf16[128,2048]{1,0:T(8,128)(2,1)S(1)} %all_gather.50) | copy-start | bytes 1572868
  237.4 186.9 %reduce-scatter.27.cloned.1.call-start = ((), (), s32[]{:S(2)}) async-start(), calls=%async_computation.19 | async-start | bytes 1310720 | tf_op jit(solution)/shard_map/reduce_scatter | solution.py:99
  312.5 0.9 copy-start
  332.8 1.0 copy-start.2
  344.8 171.6 %reduce-scatter.31.cloned.1.call-start = ((), (), s32[]{:S(2)}) async-start(), calls=%async_computation.21 | async-start | bytes 2293760 | tf_op jit(solution)/shard_map/reduce_scatter | solution.py:28
  371.6 144.7 %reduce-scatter.29.cloned.1.call-start = ((), (), s32[]{:S(2)}) async-start(), calls=%async_computation.20 | async-start | bytes 2293760 | tf_op jit(solution)/shard_map/reduce_scatter | solution.py:27
  380.3 136.1 %reduce-scatter.33.cloned.1.call-start = ((), (), s32[]{:S(2)}) async-start(), calls=%async_computation.22 | async-start | bytes 2293760 | tf_op jit(solution)/shard_map/reduce_scatter | solution.py:29
  426.1 14.3 %copy-start.11 = (bf16[2,32,2048]{2,1,0:T(8,128)(2,1)S(1)}, bf16[2,32,2048]{2,1,0:T(8,128)(2,1)}, u32[]{:S(2)}) copy-start(bf16[2,32,2048]{2,1,0:T(8,128)(2,1)} %param.7) | copy-start | bytes 786436
  426.1 14.3 %collective-permute-start.1 = (bf16[32,2048]{1,0:T(8,128)(2,1)S(1)}, bf16[32,2048]{1,0:T(8,128)(2,1)S(1)}, u32[]{:S(2)}, u32[]{:S(2)}) collective-permute-start(bf16[32,2048]{1,0:T(8,128)(2,1)S(1)} %get-tuple-element.5), channel_id=1, source_target_pairs={{16,0},{17,1},{18,2},{19,3},{20,4},{21,5},{22,6},{23,7},{24,8},{25... | collective-permute-start | bytes 393224 | tf_op jit(solution)/shard_map/ppermute | solution.py:13
  440.3 25.4 %copy-start.3 = (bf16[128,3584]{1,0:T(8,128)(2,1)S(1)}, bf16[128,3584]{1,0:T(8,128)(2,1)}, u32[]{:S(2)}) copy-start(bf16[128,3584]{1,0:T(8,128)(2,1)} %copy-done.2) | copy-start | bytes 2752516
  453.9 11.5 %copy-start.7 = (bf16[128,2048]{1,0:T(8,128)(2,1)}, bf16[128,2048]{1,0:T(8,128)(2,1)S(1)}, u32[]{:S(2)}) copy-start(bf16[128,2048]{1,0:T(8,128)(2,1)S(1)} %all_gather.54) | copy-start | bytes 1572868
  465.5 12.7 %copy-start.15 = (bf16[32,3584]{1,0:T(8,128)(2,1)S(1)}, bf16[32,3584]{1,0:T(8,128)(2,1)}, u32[]{:S(2)}) copy-start(bf16[32,3584]{1,0:T(8,128)(2,1)} %get-tuple-element.8) | copy-start | bytes 688132
  465.5 27.4 %copy-start.1 = (bf16[128,3584]{1,0:T(8,128)(2,1)S(1)}, bf16[128,3584]{1,0:T(8,128)(2,1)}, u32[]{:S(2)}) copy-start(bf16[128,3584]{1,0:T(8,128)(2,1)} %copy-done) | copy-start | bytes 2752516
  465.5 176.9 %reduce-scatter.35.cloned.1.call-start = ((), (), s32[]{:S(2)}) async-start(), calls=%async_computation.23 | async-start | bytes 1310720 | tf_op jit(solution)/shard_map/reduce_scatter | solution.py:99
  492.9 11.9 %copy-start.6 = (bf16[128,2048]{1,0:T(8,128)(2,1)S(1)}, bf16[128,2048]{1,0:T(8,128)(2,1)}, u32[]{:S(2)}) copy-start(bf16[128,2048]{1,0:T(8,128)(2,1)} %copy-done.5) | copy-start | bytes 1572868
  567.3 25.2 %copy-start.8 = (bf16[128,2048]{1,0:T(8,128)(2,1)S(1)}, bf16[128,2048]{1,0:T(8,128)(2,1)}, u32[]{:S(2)}) copy-start(bf16[128,2048]{1,0:T(8,128)(2,1)} %copy-done.7) | copy-start | bytes 1572868
  617.4 25.0 %copy-start.13 = (bf16[1,2,32,2048]{3,2,1,0:T(8,128)(2,1)S(1)}, bf16[1,2,32,2048]{3,2,1,0:T(8,128)(2,1)}, u32[]{:S(2)}) copy-start(bf16[1,2,32,2048]{3,2,1,0:T(8,128)(2,1)} %get-tuple-element.4) | copy-start | bytes 786436
  643.4 0.7 copy-start.14
Sparse Core Ops, SparseCore 0:
  32.1 32.5 reduce-scatter.14
  67.8 29.5 reduce-scatter.12
  99.9 29.5 reduce-scatter.16
  171.7 32.0 reduce-scatter.18
  206.7 28.9 reduce-scatter.22
  238.7 29.5 reduce-scatter.20
  270.8 29.5 reduce-scatter.24
  344.9 32.3 reduce-scatter.26
  380.4 28.8 reduce-scatter.30
  412.3 29.5 reduce-scatter.28
  465.6 34.4 reduce-scatter.32
  557.7 26.1 reduce-scatter.34
where the time goes:
time: 661 us; the launch traced here: 651 us
  matrix products  296 us (45%)
  blocking collectives  184 us (28%)
  waiting for transfers between devices  118 us (18%)
  local copies, waits for them, and re-layouts  22.7 us (3%)
  between operations  14.9 us (2%)
  other arithmetic  10.1 us (2%)
    reduce_scatter x3, waiting for transfers between devices, combine(): lax.psum_scatter(grad_part, 'row', scatter_dimension=0, tiled=True)  64.3 us
    reduce_scatter x3, waiting for transfers between devices, combine(): lax.psum_scatter(gate_part, 'row', scatter_dimension=0, tiled=True)  51.9 us
    all_gather x3, blocking collectives, shards(): lax.all_gather(local_input, 'col', axis=0, tiled=True)  50.5 us
    dot_general x3, matrix products, shards(): jnp.einsum('td,tf->df', rows_input, grad_hgate, preferred_element_type=jn...  49.9 us
    dot_general x3, matrix products, shards(): jnp.einsum('tf,td->fd', hidden, rows_grad, preferred_element_type=jnp.flo...  49.2 us
    dot_general x3, matrix products, shards(): jnp.einsum('td,tf->df', rows_input, grad_up, preferred_element_type=jnp.f...  48.8 us
    all_gather x3, blocking collectives, shards(): lax.all_gather(grad_in, 'col', axis=0, tiled=True)  39.3 us
    all_gather x3, blocking collectives, combine(): lax.all_gather(results[0], 'row', axis=0, tiled=True)  37.1 us
  transfers between devices with their start and end apart: 14, of which 5 were waited for; matrix products, arithmetic and copies ran while one was open for 38% of the time, Pallas kernels for 0%

commit v1 on v0

--- a/solution.py
+++ b/solution.py
@@ -5,6 +5,17 @@
 
 BLK = 64
 TB = 64
+
+
+def collect(x, axis, dim):
+    ways = lax.axis_size(axis)
+    pieces = [x]
+    for far in range(1, ways):
+        pieces.append(
+            lax.ppermute(pieces[far - 1], axis, [(d, (d - 1) % ways) for d in range(ways)])
+        )
+    line = jnp.concatenate(pieces, axis=dim)
+    return jnp.roll(line, lax.axis_index(axis) * x.shape[dim], axis=dim)
 
 
 def passed_along(value, axis, steps):
@@ -32,7 +43,7 @@
     own_mask = lax.dynamic_slice_in_dim(keep_mask, lax.axis_index("row") * row_count, row_count, 0)
     results = activate(gate_total, up_total, grad_total, own_mask)
     hidden, grad_hgate, grad_up = (
-        lax.all_gather(results[0], "row", axis=0, tiled=True),
+        collect(results[0], "row", 0),
         lax.all_gather(results[1], "row", axis=0, tiled=True),
         lax.all_gather(results[2], "row", axis=0, tiled=True),
     )

time: 661 us -> 638 us (0.965)
  blocking collectives: 184 us -> 147 us
  starting transfers between devices: 5.35 us -> 14.5 us
    all_gather x3 -> x0, blocking collectives: 37.1 us -> none  [combine(): lax.all_gather(results[0], 'row', axis=0, tiled=True)]
    ppermute x0 -> x9, starting transfers between devices: none -> 8.98 us  [collect(): lax.ppermute(pieces[far - 1], axis, [(d, (d - 1) % ways) for d in range(w...]
  transfers between devices with their start and end apart: 14 -> 23, of which waited for: 5 -> 5; matrix products, arithmetic and copies ran while one was open for 38% -> 43% of each run, Pallas kernels for 0% -> 0%
where the time goes in v1:
time: 638 us; the launch traced here: 628 us
  matrix products  299 us (47%)
  blocking collectives  147 us (23%)
  waiting for transfers between devices  116 us (18%)
  local copies, waits for them, and re-layouts  26 us (4%)
  between operations  14.9 us (2%)
  starting transfers between devices  14.5 us (2%)
  other arithmetic  10.1 us (2%)
    reduce_scatter x3, waiting for transfers between devices, combine(): lax.psum_scatter(grad_part, 'row', scatter_dimension=0, tiled=True)  64.3 us
    dot_general x3, matrix products, shards(): jnp.einsum('tf,td->fd', hidden, rows_grad, preferred_element_type=jnp.flo...  52.4 us
    all_gather x3, blocking collectives, shards(): lax.all_gather(local_input, 'col', axis=0, tiled=True)  51 us
    reduce_scatter x3, waiting for transfers between devices, combine(): lax.psum_scatter(gate_part, 'row', scatter_dimension=0, tiled=True)  49.6 us
    dot_general x3, matrix products, shards(): jnp.einsum('td,tf->df', rows_input, grad_hgate, preferred_element_type=jn...  49.5 us
    dot_general x3, matrix products, shards(): jnp.einsum('td,tf->df', rows_input, grad_up, preferred_element_type=jnp.f...  48.5 us
    all_gather x3, blocking collectives, shards(): lax.all_gather(grad_in, 'col', axis=0, tiled=True)  39.3 us
    dot_general x3, matrix products, shards(): jnp.einsum('td,fd->tf', rows_grad, w_down, preferred_element_type=jnp.flo...  34.4 us
  transfers between devices with their start and end apart: 23, of which 5 were waited for; matrix products, arithmetic and copies ran while one was open for 43% of the time, Pallas kernels for 0%

profile of v1, /device:TPU:3, one launch (start us, length us, event | category | flops | bytes accessed | tf_op | source)
XLA Modules:
  0.0 627.8 jit_solution(4371396703627289142)
XLA Ops:
  8.9 14.5 %all-gather = bf16[1,1,128,2048]{3,2,1,0:T(8,128)(2,1)S(1)} all-gather(bf16[1,1,32,2048]{3,2,1,0:T(8,128)(2,1)S(1)} %get-tuple-element.19), channel_id=2, replica_groups=mesh['section'=2,'row'=4,'col'=4] {'col'}, dimensions={2}, use_global_device_ids=true | all-gather | bytes 655360 | tf_op jit(solution)/shard_map/all_gather | solution.py:77
  23.4 8.5 %fusion.16 = f32[128,3584]{1,0:T(8,128)} fusion(bf16[1,2048,3584]{2,1,0:T(8,128)(2,1)} %param.11, bf16[1,1,128,2048]{3,2,1,0:T(8,128)(2,1)S(1)} %all-gather), kind=kOutput, calls=%fused_computation.19 | convolution fusion | flops 1879048192 | bytes 17039360 | tf_op jit(solution)/shard_map/dot_general | solution.py:92
  32.0 8.5 %fusion.28 = f32[128,3584]{1,0:T(8,128)} fusion(bf16[1,2048,3584]{2,1,0:T(8,128)(2,1)} %param.10, bf16[1,1,128,2048]{3,2,1,0:T(8,128)(2,1)S(1)} %all-gather), kind=kOutput, calls=%fused_computation.31 | convolution fusion | flops 1879048192 | bytes 17039360 | tf_op jit(solution)/shard_map/dot_general | solution.py:91
  41.5 11.9 %all-gather.1 = bf16[1,128,2048]{2,1,0:T(8,128)(2,1)S(1)} all-gather(bf16[1,32,2048]{2,1,0:T(8,128)(2,1)S(1)} %dynamic-slice_select_fusion), channel_id=3, replica_groups=mesh['section'=2,'row'=4,'col'=4] {'col'}, dimensions={1}, use_global_device_ids=true | all-gather | bytes 655360 | tf_op jit(solution)/shard_map/all_gather | solution.py:78
  54.2 11.4 %fusion.4 = f32[128,3584]{1,0:T(8,128)} fusion(bf16[1,3584,2048]{2,1,0:T(8,128)(2,1)} %param.12, bf16[1,128,2048]{2,1,0:T(8,128)(2,1)S(1)} %all-gather.1), kind=kOutput, calls=%fused_computation.7 | convolution fusion | flops 1879048192 | bytes 17039360 | tf_op jit(solution)/shard_map/td,fd->tf/dot_general | solution.py:93
  68.5 3.0 reshape.48
  71.6 25.8 %reduce-scatter.13.cloned.1.call-done = f32[32,3584]{1,0:T(8,128)} async-done(((f32[128,3584]{1,0:T(8,128)}), f32[32,3584]{1,0:T(8,128)}) %reduce-scatter.13.cloned.1.call-update) | async-done | bytes 458768 | tf_op jit(solution)/shard_map/reduce_scatter | solution.py:38
  97.4 32.2 %reduce-scatter.17.cloned.1.call-done = f32[32,3584]{1,0:T(8,128)} async-done(((f32[128,3584]{1,0:T(8,128)}), f32[32,3584]{1,0:T(8,128)}) %reduce-scatter.17.cloned.1.call-update) | async-done | bytes 458768 | tf_op jit(solution)/shard_map/reduce_scatter | solution.py:40
  131.7 9.4 %all_gather.39 = bf16[128,3584]{1,0:T(8,128)(2,1)S(1)} all-gather(bf16[32,3584]{1,0:T(8,128)(2,1)S(1)} %get-tuple-element.11), channel_id=1, replica_groups=mesh['section'=2,'row'=4,'col'=4] {'row'}, dimensions={0}, use_global_device_ids=true | all-gather | bytes 1146880 | tf_op jit(solution)/shard_map/all_gather | solution.py:48
  141.1 9.9 %fusion.14 = f32[128,2048]{1,0:T(8,128)S(1)} fusion(bf16[128,3584]{1,0:T(8,128)(2,1)S(1)} %all_gather.39, bf16[1,2048,3584]{2,1,0:T(8,128)(2,1)} %param.11), kind=kOutput, calls=%fused_computation.17 | convolution fusion | flops 1879048192 | bytes 16646144 | tf_op jit(solution)/shard_map/tf,df->td/dot_general | solution.py:107
  151.0 9.6 %all_gather.38 = bf16[128,3584]{1,0:T(8,128)(2,1)S(1)} all-gather(bf16[32,3584]{1,0:T(8,128)(2,1)S(1)} %get-tuple-element.10), channel_id=1, replica_groups=mesh['section'=2,'row'=4,'col'=4] {'row'}, dimensions={0}, use_global_device_ids=true | all-gather | bytes 1146880 | tf_op jit(solution)/shard_map/all_gather | solution.py:47
  160.6 10.9 %fusion.33 = f32[128,2048]{1,0:T(8,128)} fusion(f32[128,2048]{1,0:T(8,128)S(1)} %fusion.14, bf16[128,3584]{1,0:T(8,128)(2,1)S(1)} %all_gather.38, bf16[1,2048,3584]{2,1,0:T(8,128)(2,1)} %param.10), kind=kOutput, calls=%fused_computation.36 | convolution fusion | flops 1879310336 | bytes 17694720 | tf_op jit(solution)/shard_map/tf,df->td/dot_general | solution.py:104
  171.6 17.7 %all-gather.2 = bf16[1,1,128,2048]{3,2,1,0:T(8,128)(2,1)S(1)} all-gather(bf16[1,1,32,2048]{3,2,1,0:T(8,128)(2,1)S(1)} %get-tuple-element.20), channel_id=4, replica_groups=mesh['section'=2,'row'=4,'col'=4] {'col'}, dimensions={2}, use_global_device_ids=true | all-gather | bytes 655360 | tf_op jit(solution)/shard_map/all_gather | solution.py:77
  189.4 8.5 %fusion.12 = f32[128,3584]{1,0:T(8,128)} fusion(bf16[1,2048,3584]{2,1,0:T(8,128)(2,1)} %param.11, bf16[1,1,128,2048]{3,2,1,0:T(8,128)(2,1)S(1)} %all-gather.2), kind=kOutput, calls=%fused_computation.15 | convolution fusion | flops 1879048192 | bytes 17039360 | tf_op jit(solution)/shard_map/dot_general | solution.py:92
  198.0 8.6 %fusion.24 = f32[128,3584]{1,0:T(8,128)} fusion(bf16[1,2048,3584]{2,1,0:T(8,128)(2,1)} %param.10, bf16[1,1,128,2048]{3,2,1,0:T(8,128)(2,1)S(1)} %all-gather.2), kind=kOutput, calls=%fused_computation.27 | convolution fusion | flops 1879048192 | bytes 17039360 | tf_op jit(solution)/shard_map/dot_general | solution.py:91
  208.5 2.7 collective-permute-start
  213.2 13.4 %all_gather.41 = bf16[128,2048]{1,0:T(8,128)(2,1)S(1)} all-gather(bf16[32,2048]{1,0:T(8,128)(2,1)S(1)} %bitcast_select_fusion.2), channel_id=1, replica_groups=mesh['section'=2,'row'=4,'col'=4] {'col'}, dimensions={0}, use_global_device_ids=true | all-gather | bytes 655360 | tf_op jit(solution)/shard_map/all_gather | solution.py:78
  226.6 11.6 %fusion.2 = f32[128,3584]{1,0:T(8,128)} fusion(bf16[128,2048]{1,0:T(8,128)(2,1)S(1)} %all_gather.41, bf16[1,3584,2048]{2,1,0:T(8,128)(2,1)} %param.12), kind=kOutput, calls=%fused_computation.5 | convolution fusion | flops 1879048192 | bytes 17039360 | tf_op jit(solution)/shard_map/td,fd->tf/dot_general | solution.py:93
  238.4 2.1 broadcast_in_dim.52
  240.5 4.0 reshape.49
  244.6 23.7 %reduce-scatter.21.cloned.1.call-done = f32[32,3584]{1,0:T(8,128)} async-done(((f32[128,3584]{1,0:T(8,128)}), f32[32,3584]{1,0:T(8,128)}) %reduce-scatter.21.cloned.1.call-update) | async-done | bytes 458768 | tf_op jit(solution)/shard_map/reduce_scatter | solution.py:38
  268.3 32.2 %reduce-scatter.25.cloned.1.call-done = f32[32,3584]{1,0:T(8,128)} async-done(((f32[128,3584]{1,0:T(8,128)}), f32[32,3584]{1,0:T(8,128)}) %reduce-scatter.25.cloned.1.call-update) | async-done | bytes 458768 | tf_op jit(solution)/shard_map/reduce_scatter | solution.py:40
  300.5 2.3 multiply_convert_fusion.1
  302.7 9.8 %all_gather.43 = bf16[128,3584]{1,0:T(8,128)(2,1)S(1)} all-gather(bf16[32,3584]{1,0:T(8,128)(2,1)S(1)} %get-tuple-element.14), channel_id=1, replica_groups=mesh['section'=2,'row'=4,'col'=4] {'row'}, dimensions={0}, use_global_device_ids=true | all-gather | bytes 1146880 | tf_op jit(solution)/shard_map/all_gather | solution.py:48
  312.6 10.2 %fusion.10 = f32[128,2048]{1,0:T(8,128)S(1)} fusion(bf16[128,3584]{1,0:T(8,128)(2,1)S(1)} %all_gather.43, bf16[1,2048,3584]{2,1,0:T(8,128)(2,1)} %param.11), kind=kOutput, calls=%fused_computation.13 | convolution fusion | flops 1879048192 | bytes 16646144 | tf_op jit(solution)/shard_map/tf,df->td/dot_general | solution.py:107
  322.8 9.4 %all_gather.42 = bf16[128,3584]{1,0:T(8,128)(2,1)S(1)} all-gather(bf16[32,3584]{1,0:T(8,128)(2,1)S(1)} %get-tuple-element.13), channel_id=1, replica_groups=mesh['section'=2,'row'=4,'col'=4] {'row'}, dimensions={0}, use_global_device_ids=true | all-gather | bytes 1146880 | tf_op jit(solution)/shard_map/all_gather | solution.py:47
  333.2 11.0 %fusion.36 = f32[128,2048]{1,0:T(8,128)} fusion(f32[128,2048]{1,0:T(8,128)S(1)} %fusion.10, bf16[128,3584]{1,0:T(8,128)(2,1)S(1)} %all_gather.42, bf16[1,2048,3584]{2,1,0:T(8,128)(2,1)} %param.10), kind=kOutput, calls=%fused_computation.37 | convolution fusion | flops 1879310336 | bytes 17694720 | tf_op jit(solution)/shard_map/tf,df->td/dot_general | solution.py:104
  344.3 18.8 %all-gather.3 = bf16[1,1,128,2048]{3,2,1,0:T(8,128)(2,1)S(1)} all-gather(bf16[1,1,32,2048]{3,2,1,0:T(8,128)(2,1)} %get-tuple-element.18), channel_id=5, replica_groups=mesh['section'=2,'row'=4,'col'=4] {'col'}, dimensions={2}, use_global_device_ids=true | all-gather | bytes 655360 | tf_op jit(solution)/shard_map/all_gather | solution.py:77
  363.0 8.5 %fusion.8 = f32[128,3584]{1,0:T(8,128)} fusion(bf16[1,2048,3584]{2,1,0:T(8,128)(2,1)} %param.11, bf16[1,1,128,2048]{3,2,1,0:T(8,128)(2,1)S(1)} %all-gather.3), kind=kOutput, calls=%fused_computation.11 | convolution fusion | flops 1879048192 | bytes 17039360 | tf_op jit(solution)/shard_map/dot_general | solution.py:92
  371.6 8.6 %fusion.20 = f32[128,3584]{1,0:T(8,128)} fusion(bf16[1,2048,3584]{2,1,0:T(8,128)(2,1)} %param.10, bf16[1,1,128,2048]{3,2,1,0:T(8,128)(2,1)S(1)} %all-gather.3), kind=kOutput, calls=%fused_computation.23 | convolution fusion | flops 1879048192 | bytes 17039360 | tf_op jit(solution)/shard_map/dot_general | solution.py:91
  382.6 4.0 reshape.50
  386.6 3.2 collective-permute-start.2
  389.8 12.0 %fusion.85 = f32[2048,3584]{1,0:T(8,128)} fusion(bf16[128,3584]{1,0:T(8,128)(2,1)S(1)} %all_gather.38, bf16[1,1,128,2048]{3,2,1,0:T(8,128)(2,1)S(1)} %all-gather), kind=kOutput, calls=%fused_computation.103 | convolution fusion | flops 1879048192 | bytes 30801920 | tf_op jit(solution)/shard_map/td,tf->df/dot_general | solution.py:95
  404.6 2.3 collective-permute-start.1
  406.9 11.8 %fusion.83 = f32[2048,3584]{1,0:T(8,128)} fusion(bf16[128,3584]{1,0:T(8,128)(2,1)S(1)} %all_gather.39, bf16[1,1,128,2048]{3,2,1,0:T(8,128)(2,1)S(1)} %all-gather), kind=kOutput, calls=%fused_computation.101 | convolution fusion | flops 1879048192 | bytes 30801920 | tf_op jit(solution)/shard_map/td,tf->df/dot_general | solution.py:98
  420.0 14.0 %all_gather.45 = bf16[128,2048]{1,0:T(8,128)(2,1)S(1)} all-gather(bf16[32,2048]{1,0:T(8,128)(2,1)S(1)} %bitcast_select_fusion), channel_id=1, replica_groups=mesh['section'=2,'row'=4,'col'=4] {'col'}, dimensions={0}, use_global_device_ids=true | all-gather | bytes 655360 | tf_op jit(solution)/shard_map/all_gather | solution.py:78
  434.8 11.4 %fusion = f32[128,3584]{1,0:T(8,128)} fusion(bf16[128,2048]{1,0:T(8,128)(2,1)S(1)} %all_gather.45, bf16[1,3584,2048]{2,1,0:T(8,128)(2,1)} %param.12), kind=kOutput, calls=%fused_computation.3 | convolution fusion | flops 1879048192 | bytes 17039360 | tf_op jit(solution)/shard_map/td,fd->tf/dot_general | solution.py:93
  447.4 12.3 %fusion.77 = f32[2048,3584]{1,0:T(8,128)} fusion(bf16[128,3584]{1,0:T(8,128)(2,1)S(1)} %copy-done.3, bf16[1,1,128,2048]{3,2,1,0:T(8,128)(2,1)S(1)} %all-gather.2), kind=kOutput, calls=%fused_computation.95 | convolution fusion | flops 1879048192 | bytes 30801920 | tf_op jit(solution)/shard_map/td,tf->df/dot_general | solution.py:95
  461.7 11.8 %fusion.75 = f32[2048,3584]{1,0:T(8,128)} fusion(bf16[128,3584]{1,0:T(8,128)(2,1)S(1)} %copy-done.1, bf16[1,1,128,2048]{3,2,1,0:T(8,128)(2,1)S(1)} %all-gather.2), kind=kOutput, calls=%fused_computation.93 | convolution fusion | flops 1879048192 | bytes 30801920 | tf_op jit(solution)/shard_map/td,tf->df/dot_general | solution.py:98
  473.5 13.8 %fusion.56 = f32[3584,2048]{1,0:T(8,128)} fusion(bf16[128,2048]{1,0:T(8,128)(2,1)S(1)} %copy-done.7, s32[]{:T(128)S(6)} %select_n.106, bf16[32,3584]{1,0:T(8,128)(2,1)} %get-tuple-element.12, bf16[32,3584]{1,0:T(8,128)(2,1)} %collective-permute-done.5, bf16[32,3584]{1,0:T(8,128)(2,1)S(1)} %collective-permute-done.6, ...), kind=kOutput, calls=%fused_computation.75 | convolution fusion | flops 1886388224 | bytes 30801924 | tf_op jit(solution)/shard_map/tf,td->fd/dot_general | solution.py:101
  488.9 9.4 %all_gather.47 = bf16[128,3584]{1,0:T(8,128)(2,1)S(1)} all-gather(bf16[32,3584]{1,0:T(8,128)(2,1)S(1)} %get-tuple-element.17), channel_id=1, replica_groups=mesh['section'=2,'row'=4,'col'=4] {'row'}, dimensions={0}, use_global_device_ids=true | all-gather | bytes 1146880 | tf_op jit(solution)/shard_map/all_gather | solution.py:48
  498.3 9.9 %fusion.6 = f32[128,2048]{1,0:T(8,128)S(1)} fusion(bf16[128,3584]{1,0:T(8,128)(2,1)S(1)} %all_gather.47, bf16[1,2048,3584]{2,1,0:T(8,128)(2,1)} %param.11), kind=kOutput, calls=%fused_computation.9 | convolution fusion | flops 1879048192 | bytes 16646144 | tf_op jit(solution)/shard_map/tf,df->td/dot_general | solution.py:107
  508.2 9.4 %all_gather.46 = bf16[128,3584]{1,0:T(8,128)(2,1)S(1)} all-gather(bf16[32,3584]{1,0:T(8,128)(2,1)S(1)} %get-tuple-element.16), channel_id=1, replica_groups=mesh['section'=2,'row'=4,'col'=4] {'row'}, dimensions={0}, use_global_device_ids=true | all-gather | bytes 1146880 | tf_op jit(solution)/shard_map/all_gather | solution.py:47
  517.8 11.0 %fusion.39 = f32[128,2048]{1,0:T(8,128)} fusion(f32[128,2048]{1,0:T(8,128)S(1)} %fusion.6, bf16[128,3584]{1,0:T(8,128)(2,1)S(1)} %all_gather.46, bf16[1,2048,3584]{2,1,0:T(8,128)(2,1)} %param.10), kind=kOutput, calls=%fused_computation.38 | convolution fusion | flops 1879310336 | bytes 17694720 | tf_op jit(solution)/shard_map/tf,df->td/dot_general | solution.py:104
  529.7 25.1 %fusion.30 = bf16[1,2048,3584]{2,1,0:T(8,128)(2,1)} fusion(bf16[128,3584]{1,0:T(8,128)(2,1)S(1)} %all_gather.46, f32[2048,3584]{1,0:T(8,128)} %fusion.85, f32[2048,3584]{1,0:T(8,128)} %fusion.77, bf16[1,1,128,2048]{3,2,1,0:T(8,128)(2,1)S(1)} %all-gather.3), kind=kOutput, calls=%fused_computation.33 | convolution fusion | flops 1901068288 | bytes 74842112 | tf_op jit(solution)/shard_map/td,tf->df/dot_general | solution.py:95
  555.2 25.0 %fusion.31 = bf16[1,2048,3584]{2,1,0:T(8,128)(2,1)} fusion(bf16[128,3584]{1,0:T(8,128)(2,1)S(1)} %all_gather.47, f32[2048,3584]{1,0:T(8,128)} %fusion.83, f32[2048,3584]{1,0:T(8,128)} %fusion.75, bf16[1,1,128,2048]{3,2,1,0:T(8,128)(2,1)S(1)} %all-gather.3), kind=kOutput, calls=%fused_computation.34 | convolution fusion | flops 1901068288 | bytes 74842112 | tf_op jit(solution)/shard_map/td,tf->df/dot_general | solution.py:98
  580.2 12.5 %fusion.46 = f32[3584,2048]{1,0:T(8,128)} fusion(bf16[128,2048]{1,0:T(8,128)(2,1)S(1)} %copy-done.9, s32[]{:T(128)S(6)} %select_n.106, bf16[32,3584]{1,0:T(8,128)(2,1)S(1)} %get-tuple-element.15, bf16[32,3584]{1,0:T(8,128)(2,1)S(1)} %collective-permute-done.8, bf16[32,3584]{1,0:T(8,128)(2,1)S(1)} %collective-permute-done.9, ...), kind=kOutput, calls=%fused_computation.67 | convolution fusion | flops 1886388224 | bytes 30801924 | tf_op jit(solution)/shard_map/tf,td->fd/dot_general | solution.py:101
  592.7 26.1 %fusion.32 = bf16[1,3584,2048]{2,1,0:T(8,128)(2,1)} fusion(f32[3584,2048]{1,0:T(8,128)} %fusion.46, f32[3584,2048]{1,0:T(8,128)} %fusion.56, s32[]{:T(128)S(6)} %select_n.106, bf16[32,3584]{1,0:T(8,128)(2,1)S(1)} %copy-done.16, bf16[32,3584]{1,0:T(8,128)(2,1)} %collective-permute-done.2, bf16[32,3584]{1,0:T(8,128)(2,1)} %collective-permute-done.3, ...), kind=kOutput, calls=%fused_computation.35 | convolution fusion | flops 1908408320 | bytes 74842112 | tf_op jit(solution)/shard_map/tf,td->fd/dot_general | solution.py:101
  (106 shorter events, 29.1 us)
Async XLA Ops:
  7.2 64.4 %reduce-scatter.15.cloned.1.call-start = ((), (), s32[]{:S(2)}) async-start(), calls=%async_computation.13 | async-start | bytes 2293760 | tf_op jit(solution)/shard_map/reduce_scatter | solution.py:39
  31.9 65.4 %reduce-scatter.13.cloned.1.call-start = ((), (), s32[]{:S(2)}) async-start(), calls=%async_computation.12 | async-start | bytes 2293760 | tf_op jit(solution)/shard_map/reduce_scatter | solution.py:38
  40.5 1.0 copy-start.10
  40.5 89.1 %reduce-scatter.17.cloned.1.call-start = ((), (), s32[]{:S(2)}) async-start(), calls=%async_computation.14 | async-start | bytes 2293760 | tf_op jit(solution)/shard_map/reduce_scatter | solution.py:40
  53.4 0.8 copy-start.4
  65.6 0.7 copy-start.17
  65.6 141.0 %reduce-scatter.19.cloned.1.call-start = ((), (), s32[]{:S(2)}) async-start(), calls=%async_computation.15 | async-start | bytes 1310720 | tf_op jit(solution)/shard_map/reduce_scatter | solution.py:110
  171.6 73.0 %reduce-scatter.23.cloned.1.call-start = ((), (), s32[]{:S(2)}) async-start(), calls=%async_computation.17 | async-start | bytes 2293760 | tf_op jit(solution)/shard_map/reduce_scatter | solution.py:39
  197.9 70.4 %reduce-scatter.21.cloned.1.call-start = ((), (), s32[]{:S(2)}) async-start(), calls=%async_computation.16 | async-start | bytes 2293760 | tf_op jit(solution)/shard_map/reduce_scatter | solution.py:38
  206.5 0.9 copy-start.11
  206.6 93.9 %reduce-scatter.25.cloned.1.call-start = ((), (), s32[]{:S(2)}) async-start(), calls=%async_computation.18 | async-start | bytes 2293760 | tf_op jit(solution)/shard_map/reduce_scatter | solution.py:40
  208.5 4.7 copy-start.13
  208.5 4.6 collective-permute-start
  226.6 11.6 %copy-start.6 = (bf16[128,2048]{1,0:T(8,128)(2,1)}, bf16[128,2048]{1,0:T(8,128)(2,1)S(1)}, u32[]{:S(2)}) copy-start(bf16[128,2048]{1,0:T(8,128)(2,1)S(1)} %all_gather.41) | copy-start | bytes 1572868
  238.2 164.7 %reduce-scatter.27.cloned.1.call-start = ((), (), s32[]{:S(2)}) async-start(), calls=%async_computation.19 | async-start | bytes 1310720 | tf_op jit(solution)/shard_map/reduce_scatter | solution.py:110
  312.6 10.3 %copy-start = (bf16[128,3584]{1,0:T(8,128)(2,1)}, bf16[128,3584]{1,0:T(8,128)(2,1)S(1)}, u32[]{:S(2)}) copy-start(bf16[128,3584]{1,0:T(8,128)(2,1)S(1)} %all_gather.43) | copy-start | bytes 2752516
  332.2 1.0 copy-start.2
  344.2 143.1 %reduce-scatter.31.cloned.1.call-start = ((), (), s32[]{:S(2)}) async-start(), calls=%async_computation.21 | async-start | bytes 2293760 | tf_op jit(solution)/shard_map/reduce_scatter | solution.py:39
  371.6 115.7 %reduce-scatter.29.cloned.1.call-start = ((), (), s32[]{:S(2)}) async-start(), calls=%async_computation.20 | async-start | bytes 2293760 | tf_op jit(solution)/shard_map/reduce_scatter | solution.py:38
  380.2 107.0 %reduce-scatter.33.cloned.1.call-start = ((), (), s32[]{:S(2)}) async-start(), calls=%async_computation.22 | async-start | bytes 2293760 | tf_op jit(solution)/shard_map/reduce_scatter | solution.py:40
  386.6 15.1 %collective-permute-start.2 = (bf16[32,3584]{1,0:T(8,128)(2,1)}, bf16[32,3584]{1,0:T(8,128)(2,1)}, u32[]{:S(2)}, u32[]{:S(2)}) collective-permute-start(bf16[32,3584]{1,0:T(8,128)(2,1)} %get-tuple-element.9), channel_id=1, source_target_pairs={{0,12},{4,0},{8,4},{12,8},{1,13},{5,1},{9,5},{13,9},{2,14},{6,2},{... | collective-permute-start | bytes 688136 | tf_op jit(solution)/shard_map/ppermute | solution.py:15
  401.7 17.0 %collective-permute-start.3 = (bf16[32,3584]{1,0:T(8,128)(2,1)}, bf16[32,3584]{1,0:T(8,128)(2,1)}, u32[]{:S(2)}, u32[]{:S(2)}) collective-permute-start(bf16[32,3584]{1,0:T(8,128)(2,1)} %collective-permute-done.2), channel_id=1, source_target_pairs={{0,12},{4,0},{8,4},{12,8},{1,13},{5,1},{9,5},{13,9},{2,14},{6,2},{... | collective-permute-start | bytes 688136 | tf_op jit(solution)/shard_map/ppermute | solution.py:15
  401.7 17.3 %collective-permute-start.5 = (bf16[32,3584]{1,0:T(8,128)(2,1)}, bf16[32,3584]{1,0:T(8,128)(2,1)}, u32[]{:S(2)}, u32[]{:S(2)}) collective-permute-start(bf16[32,3584]{1,0:T(8,128)(2,1)} %get-tuple-element.12), channel_id=1, source_target_pairs={{0,12},{4,0},{8,4},{12,8},{1,13},{5,1},{9,5},{13,9},{2,14},{6,2},{... | collective-permute-start | bytes 688136 | tf_op jit(solution)/shard_map/ppermute | solution.py:15
  404.6 15.4 %copy-start.12 = (bf16[2,32,2048]{2,1,0:T(8,128)(2,1)S(1)}, bf16[2,32,2048]{2,1,0:T(8,128)(2,1)}, u32[]{:S(2)}) copy-start(bf16[2,32,2048]{2,1,0:T(8,128)(2,1)} %param.9) | copy-start | bytes 786436
  404.6 15.4 %collective-permute-start.1 = (bf16[32,2048]{1,0:T(8,128)(2,1)S(1)}, bf16[32,2048]{1,0:T(8,128)(2,1)S(1)}, u32[]{:S(2)}, u32[]{:S(2)}) collective-permute-start(bf16[32,2048]{1,0:T(8,128)(2,1)S(1)} %get-tuple-element.6), channel_id=1, source_target_pairs={{16,0},{17,1},{18,2},{19,3},{20,4},{21,5},{22,6},{23,7},{24,8},{25... | collective-permute-start | bytes 393224 | tf_op jit(solution)/shard_map/ppermute | solution.py:24
  418.7 174.0 %collective-permute-start.4 = (bf16[32,3584]{1,0:T(8,128)(2,1)}, bf16[32,3584]{1,0:T(8,128)(2,1)}, u32[]{:S(2)}, u32[]{:S(2)}) collective-permute-start(bf16[32,3584]{1,0:T(8,128)(2,1)} %collective-permute-done.3), channel_id=1, source_target_pairs={{0,12},{4,0},{8,4},{12,8},{1,13},{5,1},{9,5},{13,9},{2,14},{6,2},{... | collective-permute-start | bytes 688136 | tf_op jit(solution)/shard_map/ppermute | solution.py:15
  419.0 40.7 %collective-permute-start.6 = (bf16[32,3584]{1,0:T(8,128)(2,1)}, bf16[32,3584]{1,0:T(8,128)(2,1)S(1)}, u32[]{:S(2)}, u32[]{:S(2)}) collective-permute-start(bf16[32,3584]{1,0:T(8,128)(2,1)} %collective-permute-done.5), channel_id=1, source_target_pairs={{0,12},{4,0},{8,4},{12,8},{1,13},{5,1},{9,5},{13,9},{2,14},{6,2},{... | collective-permute-start | bytes 688136 | tf_op jit(solution)/shard_map/ppermute | solution.py:15
  434.0 0.8 copy-start.8
  446.2 1.2 copy-start.3
  446.2 15.4 %copy-start.1 = (bf16[128,3584]{1,0:T(8,128)(2,1)S(1)}, bf16[128,3584]{1,0:T(8,128)(2,1)}, u32[]{:S(2)}) copy-start(bf16[128,3584]{1,0:T(8,128)(2,1)} %copy-done) | copy-start | bytes 2752516
  446.2 172.6 %reduce-scatter.35.cloned.1.call-start = ((), (), s32[]{:S(2)}) async-start(), calls=%async_computation.23 | async-start | bytes 1310720 | tf_op jit(solution)/shard_map/reduce_scatter | solution.py:110
  459.7 13.7 %copy-start.7 = (bf16[128,2048]{1,0:T(8,128)(2,1)S(1)}, bf16[128,2048]{1,0:T(8,128)(2,1)}, u32[]{:S(2)}) copy-start(bf16[128,2048]{1,0:T(8,128)(2,1)} %copy-done.6) | copy-start | bytes 1572868
  459.7 13.7 %collective-permute-start.7 = (bf16[32,3584]{1,0:T(8,128)(2,1)S(1)}, bf16[32,3584]{1,0:T(8,128)(2,1)S(1)}, u32[]{:S(2)}, u32[]{:S(2)}) collective-permute-start(bf16[32,3584]{1,0:T(8,128)(2,1)S(1)} %collective-permute-done.6), channel_id=1, source_target_pairs={{0,12},{4,0},{8,4},{12,8},{1,13},{5,1},{9,5},{13,9},{2,14},{6,2},{... | collective-permute-start | bytes 688136 | tf_op jit(solution)/shard_map/ppermute | solution.py:15
  517.6 11.1 %collective-permute-start.8 = (bf16[32,3584]{1,0:T(8,128)(2,1)S(1)}, bf16[32,3584]{1,0:T(8,128)(2,1)S(1)}, u32[]{:S(2)}, u32[]{:S(2)}) collective-permute-start(bf16[32,3584]{1,0:T(8,128)(2,1)S(1)} %get-tuple-element.15), channel_id=1, source_target_pairs={{0,12},{4,0},{8,4},{12,8},{1,13},{5,1},{9,5},{13,9},{2,14},{6,2},{... | collective-permute-start | bytes 688136 | tf_op jit(solution)/shard_map/ppermute | solution.py:15
  528.8 26.1 %collective-permute-start.9 = (bf16[32,3584]{1,0:T(8,128)(2,1)S(1)}, bf16[32,3584]{1,0:T(8,128)(2,1)S(1)}, u32[]{:S(2)}, u32[]{:S(2)}) collective-permute-start(bf16[32,3584]{1,0:T(8,128)(2,1)S(1)} %collective-permute-done.8), channel_id=1, source_target_pairs={{0,12},{4,0},{8,4},{12,8},{1,13},{5,1},{9,5},{13,9},{2,14},{6,2},{... | collective-permute-start | bytes 688136 | tf_op jit(solution)/shard_map/ppermute | solution.py:15
  554.8 25.4 %copy-start.9 = (bf16[128,2048]{1,0:T(8,128)(2,1)S(1)}, bf16[128,2048]{1,0:T(8,128)(2,1)}, u32[]{:S(2)}) copy-start(bf16[128,2048]{1,0:T(8,128)(2,1)} %copy-done.8) | copy-start | bytes 1572868
  554.8 25.4 %collective-permute-start.10 = (bf16[32,3584]{1,0:T(8,128)(2,1)S(1)}, bf16[32,3584]{1,0:T(8,128)(2,1)S(1)}, u32[]{:S(2)}, u32[]{:S(2)}) collective-permute-start(bf16[32,3584]{1,0:T(8,128)(2,1)S(1)} %collective-permute-done.9), channel_id=1, source_target_pairs={{0,12},{4,0},{8,4},{12,8},{1,13},{5,1},{9,5},{13,9},{2,14},{6,2},{... | collective-permute-start | bytes 688136 | tf_op jit(solution)/shard_map/ppermute | solution.py:15
  580.2 12.5 %copy-start.5 = (bf16[1,128,2048]{2,1,0:T(8,128)(2,1)S(1)}, bf16[1,128,2048]{2,1,0:T(8,128)(2,1)}, u32[]{:S(2)}) copy-start(bf16[1,128,2048]{2,1,0:T(8,128)(2,1)} %copy-done.4) | copy-start | bytes 1572868
  580.2 12.5 %copy-start.16 = (bf16[32,3584]{1,0:T(8,128)(2,1)S(1)}, bf16[32,3584]{1,0:T(8,128)(2,1)}, u32[]{:S(2)}) copy-start(bf16[32,3584]{1,0:T(8,128)(2,1)} %get-tuple-element.9) | copy-start | bytes 688132
  592.7 26.1 %copy-start.14 = (bf16[1,2,32,2048]{3,2,1,0:T(8,128)(2,1)S(1)}, bf16[1,2,32,2048]{3,2,1,0:T(8,128)(2,1)}, u32[]{:S(2)}) copy-start(bf16[1,2,32,2048]{3,2,1,0:T(8,128)(2,1)} %get-tuple-element.5) | copy-start | bytes 786436
  619.8 0.7 copy-start.15
Sparse Core Ops, SparseCore 0:
  32.1 32.5 reduce-scatter.14
  67.8 29.5 reduce-scatter.12
  99.9 29.5 reduce-scatter.16
  171.7 31.9 reduce-scatter.18
  206.6 29.0 reduce-scatter.22
  238.7 29.5 reduce-scatter.20
  270.8 29.5 reduce-scatter.24
  344.3 32.3 reduce-scatter.26
  379.9 29.9 reduce-scatter.30
  412.8 30.1 reduce-scatter.28
  446.4 30.9 reduce-scatter.32
  528.9 28.1 reduce-scatter.34
